TPU v7x, 32 devices: a whole 2x2x4 slice. The times are simulated.
32 devices in a mesh: gz: 16 (over z, x, core), gy: 2 (over y).
Axes of the slice: x: 2, y: 2, z: 4, core: 2. Of those that a mesh axis runs over, the one named last changes fastest.
Arguments:
- spread_weights: float32 [64, 32768], P(None, ('gz', 'gy')), may hold values from -6 to 6
- spread_base: int32 [3, 32768], P(None, ('gz', 'gy')), may hold values from 0 to 383, as said below
- qm_base: int32 [3, 4096], P(None, ('gz', 'gy')), may hold values from 0 to 383, as said below
- qm_frac: float32 [3, 4096], P(None, ('gz', 'gy')), may hold values from 0 to 1
- qm_charge: float32 [4096], P(('gz', 'gy')), may hold values from -3 to 3
Outputs:
- qm_forces: float32 [3, 4096], P(None, ('gz', 'gy'))
Inputs may be any that keep to these rules, and one draw needn't show every extreme that they name: For point charge j let d = j // 1024, p = d // 2 and q = d % 2; then spread_base[0, j] lies in [p * 24, (p + 1) * 24) and spread_base[1, j] in [q * 192, (q + 1) * 192); spread_base[2, j] is any cell. For quantum-region atom i let d = i // 128, p = d // 2 and q = d % 2; then qm_base[0, i] lies in [p * 24, (p + 1) * 24) and qm_base[1, i] in [q * 192, (q + 1) * 192); qm_base[2, i] is any cell.
All inputs are finite; a program needn't handle non-finite values.
Results may differ from a plain program's by a relative error of at most 0.0003.
Values sent between devices are 32-bit elements; how exact they have to be, the bound alone decides.
A program may use at most 256 MiB of HBM per device.

v0:
```python
import math
import jax
import jax.numpy as jnp
from jax import lax
from jax.sharding import PartitionSpec as P

GRID = 384
ORDER = 4
SPLITTING = 0.8
HIGHEST = lax.Precision.HIGHEST


def passed_along(block, axis, distance):
    devices = range(lax.axis_size(axis))
    route = [((i - distance) % len(devices), i) for i in devices]
    return lax.ppermute(block, axis, route)


def moduli(index, points):
    signed = jnp.where(index < points // 2, index, index - points).astype(jnp.float32) / points
    spline = 2.0 / 3.0 + jnp.cos(2.0 * math.pi / points * index.astype(jnp.float32)) / 3.0
    return (signed * signed, 1.0 / (spline * spline), index == points // 2)


def influence(first, second, third, points):
    sq_one, mod_one, edge_one = moduli(first, points)
    sq_two, mod_two, edge_two = moduli(second, points)
    sq_three, mod_three, edge_three = moduli(third, points)
    total = sq_one + sq_two + sq_three
    safe = jnp.where(total > 0.0, total, 1.0)
    value = (
        mod_one
        * mod_two
        * mod_three
        * jnp.exp(-(math.pi * math.pi / (SPLITTING * SPLITTING)) * total)
        / (math.pi * safe)
    )
    keep = (total > 0.0) & jnp.logical_not(edge_one | edge_two | edge_three)
    return jnp.where(keep, value, 0.0)


def spline_weights(frac):
    remain = 1.0 - frac
    square = frac * frac
    cubed = square * frac
    values = jnp.stack(
        [
            remain * remain * remain / 6.0,
            (3.0 * cubed - 6.0 * square + 4.0) / 6.0,
            (-3.0 * cubed + 3.0 * square + 3.0 * frac + 1.0) / 6.0,
            cubed / 6.0,
        ]
    )
    slopes = jnp.stack(
        [
            -0.5 * remain * remain,
            (3.0 * square - 4.0 * frac) / 2.0,
            (-3.0 * square + 2.0 * frac + 1.0) / 2.0,
            0.5 * square,
        ]
    )
    return (values, slopes)


def angle_tables(rows_in, cols_in, points):
    product = rows_in[:, None] * cols_in[None, :] % points
    angle = 2.0 * math.pi / points * product.astype(jnp.float32)
    return (jnp.cos(angle), jnp.sin(angle))


def transform(real_part, imag_part, form, cosine, sine, sign):
    first = jnp.einsum(form, real_part, cosine, precision=HIGHEST)
    second = jnp.einsum(form, imag_part, sine, precision=HIGHEST)
    third = jnp.einsum(form, imag_part, cosine, precision=HIGHEST)
    fourth = jnp.einsum(form, real_part, sine, precision=HIGHEST)
    return (first - sign * second, third + sign * fourth)


def spread_grid(spread_weights, spread_base, z_first, y_first, z_extent, y_extent, points):
    count = spread_weights.shape[1]
    weights = spread_weights.reshape(ORDER, ORDER, ORDER, count)
    shifts = jnp.arange(ORDER, dtype=jnp.int32)
    local_z = spread_base[0] - z_first
    local_y = spread_base[1] - y_first
    plane_hits = (
        jnp.arange(z_extent, dtype=jnp.int32)[None, :, None]
        == local_z[None, None, :] + shifts[:, None, None]
    ).astype(jnp.float32)
    row_hits = (
        jnp.arange(y_extent, dtype=jnp.int32)[None, :, None]
        == local_y[None, None, :] + shifts[:, None, None]
    ).astype(jnp.float32)
    column_cells = (spread_base[2][None, :] + shifts[:, None]) % points
    column_hits = (
        jnp.arange(points, dtype=jnp.int32)[None, None, :] == column_cells[:, :, None]
    ).astype(jnp.float32)
    by_plane = jnp.sum(plane_hits[:, None, :, None, :] * weights[:, :, None, :, :], axis=0)
    placed = jnp.sum(by_plane[:, :, None, :, :] * row_hits[:, None, :, None, :], axis=0)
    charge = jnp.dot(
        placed.reshape(z_extent * y_extent, ORDER * count),
        column_hits.reshape(ORDER * count, points),
        precision=HIGHEST,
        preferred_element_type=jnp.float32,
    )
    return charge.reshape(z_extent, y_extent, points)


def line_tables(cells, values, slopes, extent):
    hits = (jnp.arange(extent, dtype=jnp.int32)[None, :, None] == cells[:, None, :]).astype(
        jnp.float32
    )
    return (jnp.sum(hits * values[:, None, :], axis=0), jnp.sum(hits * slopes[:, None, :], axis=0))


def interpolate(potential, qm_base, qm_frac, qm_charge, z_first, y_first):
    z_extent, y_extent, points = potential.shape
    count = qm_charge.shape[0]
    shifts = jnp.arange(ORDER, dtype=jnp.int32)[:, None]
    w_z, d_z = spline_weights(qm_frac[0])
    w_y, d_y = spline_weights(qm_frac[1])
    w_x, d_x = spline_weights(qm_frac[2])
    plane_w, plane_d = line_tables(qm_base[0][None, :] - z_first + shifts, w_z, d_z, z_extent)
    row_w, row_d = line_tables(qm_base[1][None, :] - y_first + shifts, w_y, d_y, y_extent)
    column_w, column_d = line_tables((qm_base[2][None, :] + shifts) % points, w_x, d_x, points)
    along_x = jnp.dot(
        potential.reshape(z_extent * y_extent, points),
        jnp.concatenate([column_w, column_d], axis=1),
        precision=HIGHEST,
        preferred_element_type=jnp.float32,
    ).reshape(z_extent, y_extent, 2, count)
    plain = along_x[:, :, 0, :]
    sloped = along_x[:, :, 1, :]
    force_z = jnp.sum(plain * plane_d[:, None, :] * row_w[None, :, :], axis=(0, 1))
    force_y = jnp.sum(plain * plane_w[:, None, :] * row_d[None, :, :], axis=(0, 1))
    force_x = jnp.sum(sloped * plane_w[:, None, :] * row_w[None, :, :], axis=(0, 1))
    return jnp.stack([-qm_charge * force_z, -qm_charge * force_y, -qm_charge * force_x])


def shards(spread_weights, spread_base, qm_base, qm_frac, qm_charge):
    points = GRID
    margin = ORDER - 1
    count_z = lax.axis_size("gz")
    count_y = lax.axis_size("gy")
    z_local = points // count_z
    y_local = points // count_y
    z_extent = z_local + margin
    y_extent = y_local + margin
    z_first = lax.axis_index("gz") * z_local
    y_first = lax.axis_index("gy") * y_local
    charge = spread_grid(spread_weights, spread_base, z_first, y_first, z_extent, y_extent, points)
    spill_rows = passed_along(charge[:, y_local:, :], "gy", 1)
    charge = charge[:, :y_local, :].at[:, :margin, :].add(spill_rows)
    spill_planes = passed_along(charge[z_local:], "gz", 1)
    charge = charge[:z_local].at[:margin].add(spill_planes)
    kx_count = points // 2
    kx_weight = jnp.where(jnp.arange(kx_count, dtype=jnp.int32) == 0, 1.0, 2.0).astype(jnp.float32)
    positions = jnp.arange(points, dtype=jnp.int32)
    cos_x, sin_x = angle_tables(positions, jnp.arange(kx_count, dtype=jnp.int32), points)
    real_x = jnp.einsum("zyx,xk->kyz", charge, cos_x, precision=HIGHEST)
    imag_x = -jnp.einsum("zyx,xk->kyz", charge, sin_x, precision=HIGHEST)
    packed = jnp.stack([real_x, imag_x]).reshape(2, kx_count, y_local * z_local)
    moved = lax.all_to_all(packed, "gy", split_axis=1, concat_axis=2, tiled=True)
    kx_local = kx_count // count_y
    lines = moved.reshape(2, kx_local, count_y, y_local, z_local)
    lines = lines.reshape(2, kx_local, points, z_local)
    cos_full, sin_full = angle_tables(positions, positions, points)
    real_y, imag_y = transform(lines[0], lines[1], "xyz,yk->kzx", cos_full, sin_full, -1.0)
    packed = jnp.stack([real_y, imag_y]).reshape(2, points, z_local * kx_local)
    moved = lax.all_to_all(packed, "gz", split_axis=1, concat_axis=2, tiled=True)
    ky_local = points // count_z
    lines = moved.reshape(2, ky_local, count_z, z_local, kx_local)
    lines = lines.reshape(2, ky_local, points, kx_local)
    real_z, imag_z = transform(lines[0], lines[1], "yzx,zk->yxk", cos_full, sin_full, -1.0)
    ky_index = lax.axis_index("gz") * ky_local + jnp.arange(ky_local, dtype=jnp.int32)
    kx_index = lax.axis_index("gy") * kx_local + jnp.arange(kx_local, dtype=jnp.int32)
    green = influence(
        positions[None, None, :], ky_index[:, None, None], kx_index[None, :, None], points
    )
    real_z = real_z * green
    imag_z = imag_z * green
    z_rows = (
        (
            jnp.arange(count_z, dtype=jnp.int32)[:, None] * z_local
            + jnp.arange(z_local, dtype=jnp.int32)[None, :]
        )
        % points
    ).reshape(-1)
    cos_z, sin_z = angle_tables(positions, z_rows, points)
    back_real, back_imag = transform(real_z, imag_z, "yxk,kp->pyx", cos_z, sin_z, 1.0)
    packed = jnp.stack([back_real, back_imag]).reshape(2, count_z * z_local, ky_local * kx_local)
    moved = lax.all_to_all(packed, "gz", split_axis=1, concat_axis=2, tiled=True).reshape(
        2, z_local, points, kx_local
    )
    y_rows = (
        (
            jnp.arange(count_y, dtype=jnp.int32)[:, None] * y_local
            + jnp.arange(y_local, dtype=jnp.int32)[None, :]
        )
        % points
    ).reshape(-1)
    cos_y, sin_y = angle_tables(positions, y_rows, points)
    back_real, back_imag = transform(moved[0], moved[1], "zkx,kp->pxz", cos_y, sin_y, 1.0)
    packed = jnp.stack([back_real, back_imag]).reshape(2, count_y * y_local, kx_local * z_local)
    moved = lax.all_to_all(packed, "gy", split_axis=1, concat_axis=2, tiled=True).reshape(
        2, y_local, kx_count, z_local
    )
    scale = 1.0 / float(points * points * points)
    potential = (
        jnp.einsum("ykz,xk->zyx", moved[0], cos_x * kx_weight[None, :], precision=HIGHEST)
        - jnp.einsum("ykz,xk->zyx", moved[1], sin_x * kx_weight[None, :], precision=HIGHEST)
    ) * scale
    rim_rows = passed_along(potential[:, :margin, :], "gy", -1)
    potential = jnp.concatenate([potential, rim_rows], axis=1)
    rim_planes = passed_along(potential[:margin], "gz", -1)
    potential = jnp.concatenate([potential, rim_planes], axis=0)
    return interpolate(potential, qm_base, qm_frac, qm_charge, z_first, y_first)


def solution(mesh):
    in_specs = (
        P(None, ("gz", "gy")),
        P(None, ("gz", "gy")),
        P(None, ("gz", "gy")),
        P(None, ("gz", "gy")),
        P(("gz", "gy")),
    )
    out_specs = P(None, ("gz", "gy"))
    return jax.shard_map(shards, mesh=mesh, in_specs=in_specs, out_specs=out_specs, check_vma=False)
```

profile of v0, /device:TPU:0, one launch (start us, length us, event | category | flops | bytes accessed | tf_op | source)
XLA Modules:
  0.0 1281.5 jit_solution(2450267871987228641)
XLA Ops:
  7.1 158.1 %multiply_reduce_fusion = f32[27,195,4,1024]{3,2,1,0:T(4,128)} fusion(f32[4,195,1024]{2,1,0:T(8,128)S(1)} %fusion.18, f32[4,27,4,1024]{3,2,1,0:T(4,128)S(1)} %multiply_reduce_fusion.1), kind=kLoop, calls=%fused_computation | loop fusion | flops 150958080 | bytes 91226112 | tf_op jit(solution)/shard_map/reduce_sum | solution.py:98
  165.2 75.9 %dot_general.72 = f32[27,195,4096]{2,1,0:T(8,128)} reshape(f32[27,195,4,1024]{3,2,1,0:T(4,128)} %multiply_reduce_fusion) | data formatting | bytes 172523520 | tf_op jit(solution)/shard_map/dot_general | solution.py:99
  242.2 73.9 %fusion.6 = f32[27,195,384]{2,1,0:T(8,128)S(1)} fusion(f32[27,195,4096]{2,1,0:T(8,128)} %dot_general.72, pred[4096,384,1]{1,0,2:T(32,128)(4,1)S(1)} %fusion.280), kind=kOutput, calls=%fused_computation.18 | convolution fusion | flops 99373547520 | bytes 95921664 | tf_op jit(solution)/shard_map/dot_general | solution.py:99
  332.1 11.5 collective-permute-done.1
  344.8 9.8 convolution_bitcast_fusion
  354.7 9.7 negate_bitcast_fusion
  374.1 11.4 copy.108
  385.5 80.2 %all_to_all.60 = f32[2,192,4608]{2,0,1:T(2,128)S(1)} all-to-all(f32[2,192,4608]{2,0,1:T(2,128)} %copy.108), channel_id=1, replica_groups=mesh['gz'=16,'gy'=2] {'gy'}, dimensions={1} | all-to-all | bytes 14155776 | tf_op jit(solution)/shard_map/all_to_all | solution.py:162
  476.6 10.3 fusion.44
  487.0 5.5 copy.112
  492.5 5.8 copy.113
  498.3 13.8 %fusion.42 = f32[384,96,24]{0,1,2:T(8,128)} fusion(f32[96,384,24]{1,0,2:T(8,128)} %copy.113), kind=kOutput, calls=%fused_computation.74 | convolution fusion | flops 4078190592 | bytes 7077888 | tf_op jit(solution)/shard_map/xyz,yk->kzx/dot_general | solution.py:74
  512.1 10.8 multiply_subtract_fusion
  522.9 8.9 copy.116
  531.8 14.2 %multiply_add_fusion = f32[384,96,24]{0,1,2:T(8,128)} fusion(f32[384,96,24]{0,1,2:T(8,128)} %fusion.42, f32[96,384,24]{1,0,2:T(8,128)S(1)} %copy.111), kind=kOutput, calls=%fused_computation.34 | convolution fusion | flops 4079960064 | bytes 10616832 | tf_op jit(solution)/shard_map/xyz,yk->kzx/dot_general | solution.py:75
  546.0 9.1 copy.117
  555.1 11.2 pad_maximum_fusion.1
  566.4 5.3 all-to-all-start.1
  574.6 124.7 %all-to-all-done.1 = f32[2,384,2304]{2,0,1:T(2,128)} async-done(((f32[2,384,2304]{2,0,1:T(2,128)}), f32[2,384,2304]{2,0,1:T(2,128)}, u32[]{:S(2)}, u32[]{:S(2)}) %all-to-all-start.1) | async-done | bytes 7077920 | tf_op jit(solution)/shard_map/all_to_all | solution.py:169
  706.3 6.2 squeeze.37
  712.5 15.8 %fusion.40 = f32[24,96,384]{2,1,0:T(8,128)} fusion(f32[24,384,96]{2,1,0:T(8,128)} %squeeze.37), kind=kOutput, calls=%fused_computation.72 | convolution fusion | flops 4078190592 | bytes 7077888 | tf_op jit(solution)/shard_map/yzx,zk->yxk/dot_general | solution.py:72
  731.1 6.4 squeeze.38
  737.6 15.0 %fusion.38 = f32[24,96,384]{2,1,0:T(8,128)S(1)} fusion(f32[24,384,96]{2,1,0:T(8,128)} %squeeze.38), kind=kOutput, calls=%fused_computation.70 | convolution fusion | flops 4078190592 | bytes 7077888 | tf_op jit(solution)/shard_map/yzx,zk->yxk/dot_general | solution.py:74
  752.6 14.8 %subtract_multiply_fusion = f32[24,96,384]{2,1,0:T(8,128)S(1)} fusion(f32[24,96,384]{2,1,0:T(8,128)S(1)} %copy-done.9, f32[24,384,96]{2,1,0:T(8,128)} %squeeze.38, f32[96]{0:T(128)S(1)} %copy-done.41, f32[24,384]{1,0:T(8,128)S(1)} %copy-done.11, pred[96]{0:T(512)(128)(4,1)S(1)} %copy-done.42, pred[24,384]{1,0:T(8,128)(4,1)S(1)} %broadcast_or_fusion, ...), kind=kOutput, calls=%fused_computation.33 | convolution fusion | flops 4091461632 | bytes 10700640 | tf_op jit(solution)/shard_map/yzx,zk->yxk/dot_general | solution.py:73
  767.5 12.5 add_multiply_fusion.1
  779.9 9.2 fusion.48
  789.2 10.7 fusion.46
  799.9 10.7 convolution_subtract_fusion
  810.6 8.9 copy.125
  819.5 13.8 %convolution_add_fusion = f32[384,24,96]{0,2,1:T(8,128)} fusion(f32[384,24,96]{0,2,1:T(8,128)} %fusion.46, f32[24,96,384]{2,1,0:T(8,128)S(1)} %subtract_multiply_fusion, s32[384]{0:T(512)S(1)} %add_select_fusion.7), kind=kOutput, calls=%fused_computation.47 | convolution fusion | flops 4079075328 | bytes 10618368 | tf_op jit(solution)/shard_map/yxk,kp->pyx/dot_general | solution.py:75
  833.3 9.3 copy.126
  842.6 11.2 pad_maximum_fusion.2
  853.9 31.3 %all-to-all-start.2 = ((f32[2,384,2304]{2,0,1:T(2,128)}), f32[2,384,2304]{2,0,1:T(2,128)}, u32[]{:S(2)}, u32[]{:S(2)}) async-start(f32[2,384,2304]{2,0,1:T(2,128)} %pad_maximum_fusion.2), calls=%async_computation.2 | async-start | bytes 14155776 | tf_op jit(solution)/shard_map/all_to_all | solution.py:191
  885.3 127.6 %all-to-all-done.2 = f32[2,384,2304]{2,0,1:T(2,128)} async-done(((f32[2,384,2304]{2,0,1:T(2,128)}), f32[2,384,2304]{2,0,1:T(2,128)}, u32[]{:S(2)}, u32[]{:S(2)}) %all-to-all-start.2) | async-done | bytes 7077920 | tf_op jit(solution)/shard_map/all_to_all | solution.py:191
  1028.6 10.3 fusion.80
  1038.8 10.4 fusion.74
  1058.8 9.3 fusion.76
  1068.1 9.7 fusion.78
  1086.2 12.3 copy.136
  1098.6 6.8 all-to-all-start.3
  1107.2 77.8 %all-to-all-done.3 = f32[2,384,2304]{2,0,1:T(2,128)} async-done(((f32[2,384,2304]{2,0,1:T(2,128)}), f32[2,384,2304]{2,0,1:T(2,128)}, u32[]{:S(2)}, u32[]{:S(2)}) %all-to-all-start.3) | async-done | bytes 7077920 | tf_op jit(solution)/shard_map/all_to_all | solution.py:204
  1190.9 5.5 copy.140
  1200.0 12.9 %fusion.8 = f32[384,192,24]{0,1,2:T(8,128)S(1)} fusion(f32[192,192,24]{0,2,1:T(8,128)} %bitcast.186, f32[192]{0:T(256)S(1)} %compare_select_fusion.3), kind=kOutput, calls=%fused_computation.19 | convolution fusion | flops 4077600768 | bytes 10617600 | tf_op jit(solution)/shard_map/ykz,xk->zyx/dot_general | solution.py:210
  1213.0 10.8 multiply_bitcast_fusion
  1224.2 5.6 collective-permute-done.2
  1229.9 27.0 %collective-permute-start.3 = (f32[3,195,384]{2,1,0:T(8,128)S(1)}, f32[3,195,384]{2,1,0:T(8,128)S(1)}, u32[]{:S(2)}, u32[]{:S(2)}) collective-permute-start(f32[3,195,384]{2,1,0:T(8,128)S(1)} %pad_maximum_fusion.4), channel_id=1, source_target_pairs={{2,0},{4,2},{6,4},{8,6},{10,8},{12,10},{14,12},{16,14},{18,16},{20... | collective-permute-start | bytes 2695688 | tf_op jit(solution)/shard_map/ppermute | solution.py:16
  1258.1 9.8 collective-permute-done.3
  1267.9 11.8 fusion
  (177 shorter events, 106.7 us)
Async XLA Ops:
  165.2 75.9 %copy-start.12 = (s32[1,1024]{1,0:T(1,128)S(1)}, s32[1,1024]{1,0:T(1,128)}, u32[]{:S(2)}) copy-start(s32[1,1024]{1,0:T(1,128)} %get-tuple-element.46) | copy-start | bytes 12292
  316.1 7.3 collective-permute-start
  328.3 15.2 %collective-permute-start.1 = (f32[3,192,384]{2,1,0:T(8,128)S(1)}, f32[3,192,384]{2,1,0:T(8,128)S(1)}, u32[]{:S(2)}, u32[]{:S(2)}) collective-permute-start(f32[3,192,384]{2,1,0:T(8,128)S(1)} %slice.168), channel_id=1, source_target_pairs={{30,0},{0,2},{2,4},{4,6},{6,8},{8,10},{10,12},{12,14},{14,16},{16,... | collective-permute-start | bytes 2654216 | tf_op jit(solution)/shard_map/ppermute | solution.py:16
  498.2 13.8 %copy-start.1 = (f32[96,384,24]{1,0,2:T(8,128)S(1)}, f32[96,384,24]{1,0,2:T(8,128)}, u32[]{:S(2)}) copy-start(f32[96,384,24]{1,0,2:T(8,128)} %copy.113) | copy-start | bytes 10616836
  498.2 13.8 %copy-start.2 = (f32[384,96,24]{0,1,2:T(8,128)S(1)}, f32[384,96,24]{0,1,2:T(8,128)}, u32[]{:S(2)}) copy-start(f32[384,96,24]{0,1,2:T(8,128)} %fusion.44) | copy-start | bytes 10616836
  546.0 9.1 copy-start.6
  566.4 133.0 %all-to-all-start.1 = ((f32[2,384,2304]{2,0,1:T(2,128)}), f32[2,384,2304]{2,0,1:T(2,128)}, u32[]{:S(2)}, u32[]{:S(2)}) async-start(f32[2,384,2304]{2,0,1:T(2,128)} %pad_maximum_fusion.1), calls=%async_computation.1 | async-start | bytes 14155776 | tf_op jit(solution)/shard_map/all_to_all | solution.py:169
  737.5 15.1 %copy-start.9 = (f32[24,96,384]{2,1,0:T(8,128)S(1)}, f32[24,96,384]{2,1,0:T(8,128)}, u32[]{:S(2)}) copy-start(f32[24,96,384]{2,1,0:T(8,128)} %fusion.40) | copy-start | bytes 10616836
  737.5 15.1 %copy-start.10 = (f32[24,384]{1,0:T(8,128)S(1)}, f32[24,384]{1,0:T(8,128)}, u32[]{:S(2)}) copy-start(f32[24,384]{1,0:T(8,128)} %broadcast_add_fusion) | copy-start | bytes 110596
  737.5 15.1 %copy-start.11 = (f32[24,384]{1,0:T(8,128)S(1)}, f32[24,384]{1,0:T(8,128)}, u32[]{:S(2)}) copy-start(f32[24,384]{1,0:T(8,128)} %broadcast_multiply_fusion) | copy-start | bytes 110596
  737.5 15.1 %copy-start.40 = (f32[96]{0:T(128)S(1)}, f32[96]{0:T(128)}, u32[]{:S(2)}) copy-start(f32[96]{0:T(128)} %get-tuple-element.81) | copy-start | bytes 1156
  737.5 15.1 %copy-start.41 = (f32[96]{0:T(128)S(1)}, f32[96]{0:T(128)}, u32[]{:S(2)}) copy-start(f32[96]{0:T(128)} %get-tuple-element.82) | copy-start | bytes 1156
  737.5 15.1 %copy-start.42 = (pred[96]{0:T(512)(128)(4,1)S(1)}, pred[96]{0:T(512)(128)(4,1)}, u32[]{:S(2)}) copy-start(pred[96]{0:T(512)(128)(4,1)} %fusion.189) | copy-start | bytes 292
  737.5 29.9 %slice-start = ((s8[4718592]{0:T(1024)(128)(4,1)}), s8[4194304]{0:T(1024)(128)(4,1)S(1)}, s32[]{:S(2)}) async-start(s8[4718592]{0:T(1024)(128)(4,1)} %bitcast.187), calls=%async_computation.4 | async-start | bytes 8388608
  752.6 14.8 %slice-start.1 = ((s8[4718592]{0:T(1024)(128)(4,1)}), s8[524288]{0:T(1024)(128)(4,1)S(1)}, s32[]{:S(2)}) async-start(s8[4718592]{0:T(1024)(128)(4,1)} %bitcast.187), calls=%async_computation.5 | async-start | bytes 1048576
  833.3 9.3 copy-start.5
  853.9 159.0 %all-to-all-start.2 = ((f32[2,384,2304]{2,0,1:T(2,128)}), f32[2,384,2304]{2,0,1:T(2,128)}, u32[]{:S(2)}, u32[]{:S(2)}) async-start(f32[2,384,2304]{2,0,1:T(2,128)} %pad_maximum_fusion.2), calls=%async_computation.2 | async-start | bytes 14155776 | tf_op jit(solution)/shard_map/all_to_all | solution.py:191
  1038.8 10.4 copy-start.4
  1068.1 9.7 copy-start.8
  1098.6 7.4 copy-start.13
  1098.6 86.5 %all-to-all-start.3 = ((f32[2,384,2304]{2,0,1:T(2,128)}), f32[2,384,2304]{2,0,1:T(2,128)}, u32[]{:S(2)}, u32[]{:S(2)}) async-start(f32[2,384,2304]{2,0,1:T(2,128)} %copy.136), calls=%async_computation.3 | async-start | bytes 14155776 | tf_op jit(solution)/shard_map/all_to_all | solution.py:204
  1200.0 12.9 %copy-start.3 = (f32[1,192,2,2304]{1,3,2,0:T(8,128)S(1)}, f32[1,192,2,2304]{1,3,2,0:T(8,128)}, u32[]{:S(2)}) copy-start(f32[1,192,2,2304]{1,3,2,0:T(8,128)} %copy.138) | copy-start | bytes 10616836
  1212.9 11.0 copy-start.29
  1213.0 11.0 copy-start.30
  1213.0 11.0 copy-start.31
  1213.0 11.0 copy-start.32
  1213.0 11.0 copy-start.33
  1213.0 11.0 copy-start.34
  1213.0 11.0 copy-start.35
  1213.0 11.0 copy-start.36
  1223.9 5.9 collective-permute-start.2
  1224.1 33.2 %copy-start.16 = (f32[1,128]{1,0:T(1,128)S(1)}, f32[1,128]{1,0:T(1,128)}, u32[]{:S(2)}) copy-start(f32[1,128]{1,0:T(1,128)} %get-tuple-element.71) | copy-start | bytes 1540
  1224.1 33.2 %copy-start.22 = (f32[1,128]{1,0:T(1,128)S(1)}, f32[1,128]{1,0:T(1,128)}, u32[]{:S(2)}) copy-start(f32[1,128]{1,0:T(1,128)} %get-tuple-element.57) | copy-start | bytes 1540
  1224.1 33.2 %copy-start.23 = (f32[1,128]{1,0:T(1,128)S(1)}, f32[1,128]{1,0:T(1,128)}, u32[]{:S(2)}) copy-start(f32[1,128]{1,0:T(1,128)} %get-tuple-element.58) | copy-start | bytes 1540
  1224.1 33.2 %copy-start.24 = (f32[1,128]{1,0:T(1,128)S(1)}, f32[1,128]{1,0:T(1,128)}, u32[]{:S(2)}) copy-start(f32[1,128]{1,0:T(1,128)} %get-tuple-element.59) | copy-start | bytes 1540
  1224.1 33.2 %copy-start.25 = (f32[1,128]{1,0:T(1,128)S(1)}, f32[1,128]{1,0:T(1,128)}, u32[]{:S(2)}) copy-start(f32[1,128]{1,0:T(1,128)} %get-tuple-element.63) | copy-start | bytes 1540
  1224.1 33.2 %copy-start.26 = (f32[1,128]{1,0:T(1,128)S(1)}, f32[1,128]{1,0:T(1,128)}, u32[]{:S(2)}) copy-start(f32[1,128]{1,0:T(1,128)} %get-tuple-element.64) | copy-start | bytes 1540
  1224.1 33.2 %copy-start.27 = (f32[1,128]{1,0:T(1,128)S(1)}, f32[1,128]{1,0:T(1,128)}, u32[]{:S(2)}) copy-start(f32[1,128]{1,0:T(1,128)} %get-tuple-element.65) | copy-start | bytes 1540
  1224.1 33.2 %copy-start.28 = (f32[1,128]{1,0:T(1,128)S(1)}, f32[1,128]{1,0:T(1,128)}, u32[]{:S(2)}) copy-start(f32[1,128]{1,0:T(1,128)} %get-tuple-element.66) | copy-start | bytes 1540
  1224.1 33.2 %copy-start.14 = (f32[1,128]{1,0:T(1,128)S(1)}, f32[1,128]{1,0:T(1,128)}, u32[]{:S(2)}) copy-start(f32[1,128]{1,0:T(1,128)} %get-tuple-element.73) | copy-start | bytes 1540
  1224.1 33.2 %copy-start.15 = (f32[1,128]{1,0:T(1,128)S(1)}, f32[1,128]{1,0:T(1,128)}, u32[]{:S(2)}) copy-start(f32[1,128]{1,0:T(1,128)} %get-tuple-element.75) | copy-start | bytes 1540
  1224.2 33.2 %copy-start.17 = (f32[1,128]{1,0:T(1,128)S(1)}, f32[1,128]{1,0:T(1,128)}, u32[]{:S(2)}) copy-start(f32[1,128]{1,0:T(1,128)} %get-tuple-element.49) | copy-start | bytes 1540
  1224.2 33.2 %copy-start.18 = (f32[1,128]{1,0:T(1,128)S(1)}, f32[1,128]{1,0:T(1,128)}, u32[]{:S(2)}) copy-start(f32[1,128]{1,0:T(1,128)} %get-tuple-element.60) | copy-start | bytes 1540
  1224.2 33.2 %copy-start.19 = (f32[1,128]{1,0:T(1,128)S(1)}, f32[1,128]{1,0:T(1,128)}, u32[]{:S(2)}) copy-start(f32[1,128]{1,0:T(1,128)} %get-tuple-element.61) | copy-start | bytes 1540
  1224.2 33.2 %copy-start.20 = (f32[1,128]{1,0:T(1,128)S(1)}, f32[1,128]{1,0:T(1,128)}, u32[]{:S(2)}) copy-start(f32[1,128]{1,0:T(1,128)} %get-tuple-element.62) | copy-start | bytes 1540
  1224.2 33.2 %copy-start.21 = (f32[1,128]{1,0:T(1,128)S(1)}, f32[1,128]{1,0:T(1,128)}, u32[]{:S(2)}) copy-start(f32[1,128]{1,0:T(1,128)} %get-tuple-element.67) | copy-start | bytes 1540
  1224.2 33.3 %copy-start.37 = (s32[128]{0:T(128)S(1)}, s32[128]{0:T(128)}, u32[]{:S(2)}) copy-start(s32[128]{0:T(128)} %get-tuple-element.68) | copy-start | bytes 1540
  1229.9 38.0 %collective-permute-start.3 = (f32[3,195,384]{2,1,0:T(8,128)S(1)}, f32[3,195,384]{2,1,0:T(8,128)S(1)}, u32[]{:S(2)}, u32[]{:S(2)}) collective-permute-start(f32[3,195,384]{2,1,0:T(8,128)S(1)} %pad_maximum_fusion.4), channel_id=1, source_target_pairs={{2,0},{4,2},{6,4},{8,6},{10,8},{12,10},{14,12},{16,14},{18,16},{20... | collective-permute-start | bytes 2695688 | tf_op jit(solution)/shard_map/ppermute | solution.py:16
  (4 other events, 15.8 us)
where the time goes:
time: 1290 us; the launch traced here: 1280 us
  waiting for transfers between devices  357 us (28%)
  matrix products  320 us (25%)
  local copies, waits for them, and re-layouts  245 us (19%)
  other arithmetic  205 us (16%)
  blocking collectives  80.2 us (6%)
  starting transfers between devices  73.5 us (6%)
    all_to_all x2, waiting for transfers between devices, shards(): lax.all_to_all(packed, 'gz', split_axis=1, concat_axis=2, tiled=True)  252 us
    reduce_sum x1, other arithmetic, spread_grid(): jnp.sum(by_plane[:, :, None, :, :] * row_hits[:, None, :, None, :], axis=0)  158 us
    all_to_all x1, blocking collectives, shards(): lax.all_to_all(packed, 'gy', split_axis=1, concat_axis=2, tiled=True)  80.2 us
    all_to_all x1, waiting for transfers between devices, shards(): lax.all_to_all(packed, 'gy', split_axis=1, concat_axis=2, tiled=True)  77.8 us
    dot_general x1, local copies, waits for them, and re-layouts, spread_grid(): jnp.dot(placed.reshape(z_extent * y_extent, ORDER * count), column_hits.r...  75.9 us
    dot_general x1, matrix products, spread_grid(): jnp.dot(placed.reshape(z_extent * y_extent, ORDER * count), column_hits.r...  73.9 us
    dot_general x3, matrix products, transform(): fourth = jnp.einsum(form, real_part, sine, precision=HIGHEST)  40.4 us
    unnamed x4, matrix products  39.6 us
  transfers between devices with their start and end apart: 7, of which 7 were waited for; matrix products, arithmetic and copies ran while one was open for 1% of the time, Pallas kernels for 0%

commit v1 on v0

--- a/solution.py
+++ b/solution.py
@@ -166,7 +166,10 @@
     cos_full, sin_full = angle_tables(positions, positions, points)
     real_y, imag_y = transform(lines[0], lines[1], "xyz,yk->kzx", cos_full, sin_full, -1.0)
     packed = jnp.stack([real_y, imag_y]).reshape(2, points, z_local * kx_local)
-    moved = lax.all_to_all(packed, "gz", split_axis=1, concat_axis=2, tiled=True)
+    moved = jnp.concatenate(
+        lax.all_to_all(jnp.stack(jnp.split(packed, lax.axis_size("gz"), axis=1)), "gz", 0, 0),
+        axis=2,
+    )
     ky_local = points // count_z
     lines = moved.reshape(2, ky_local, count_z, z_local, kx_local)
     lines = lines.reshape(2, ky_local, points, kx_local)

time: 1290 us -> 1280 us (level)
    all_to_all x0 -> x1, waiting for transfers between devices: none -> 125 us  [shards(): lax.all_to_all(jnp.stack(jnp.split(packed, lax.axis_size('gz'), axis=1)),...]
    all_to_all x2 -> x1, waiting for transfers between devices: 252 us -> 128 us  [shards(): lax.all_to_all(packed, 'gz', split_axis=1, concat_axis=2, tiled=True)]
    unnamed x1 -> x16, other arithmetic: 0.01 us -> 13.3 us
    all_to_all x2 -> x1, starting transfers between devices: 36.5 us -> 31.3 us  [shards(): lax.all_to_all(packed, 'gz', split_axis=1, concat_axis=2, tiled=True)]
where the time goes in v1:
time: 1280 us; the launch traced here: 1270 us
  waiting for transfers between devices  357 us (28%)
  matrix products  317 us (25%)
  local copies, waits for them, and re-layouts  233 us (18%)
  other arithmetic  208 us (16%)
  blocking collectives  80.2 us (6%)
  starting transfers between devices  73.3 us (6%)
    reduce_sum x1, other arithmetic, spread_grid(): jnp.sum(by_plane[:, :, None, :, :] * row_hits[:, None, :, None, :], axis=0)  158 us
    all_to_all x1, waiting for transfers between devices, shards(): lax.all_to_all(packed, 'gz', split_axis=1, concat_axis=2, tiled=True)  128 us
    all_to_all x1, waiting for transfers between devices, shards(): lax.all_to_all(jnp.stack(jnp.split(packed, lax.axis_size('gz'), axis=1)),...  125 us
    all_to_all x1, blocking collectives, shards(): lax.all_to_all(packed, 'gy', split_axis=1, concat_axis=2, tiled=True)  80.2 us
    all_to_all x1, waiting for transfers between devices, shards(): lax.all_to_all(packed, 'gy', split_axis=1, concat_axis=2, tiled=True)  77.8 us
    dot_general x1, local copies, waits for them, and re-layouts, spread_grid(): jnp.dot(placed.reshape(z_extent * y_extent, ORDER * count), column_hits.r...  75.9 us
    dot_general x1, matrix products, spread_grid(): jnp.dot(placed.reshape(z_extent * y_extent, ORDER * count), column_hits.r...  73.9 us
    dot_general x3, matrix products, transform(): fourth = jnp.einsum(form, real_part, sine, precision=HIGHEST)  40.5 us
  transfers between devices with their start and end apart: 7, of which 7 were waited for; matrix products, arithmetic and copies ran while one was open for 1% of the time, Pallas kernels for 0%

profile of v1, /device:TPU:0, one launch (start us, length us, event | category | flops | bytes accessed | tf_op | source)
XLA Modules:
  0.0 1269.4 jit_solution(15730643072253990759)
XLA Ops:
  7.1 158.1 %multiply_reduce_fusion = f32[27,195,4,1024]{3,2,1,0:T(4,128)} fusion(f32[4,195,1024]{2,1,0:T(8,128)S(1)} %fusion.18, f32[4,27,4,1024]{3,2,1,0:T(4,128)S(1)} %multiply_reduce_fusion.1), kind=kLoop, calls=%fused_computation | loop fusion | flops 150958080 | bytes 91226112 | tf_op jit(solution)/shard_map/reduce_sum | solution.py:98
  165.2 75.9 %dot_general.72 = f32[27,195,4096]{2,1,0:T(8,128)} reshape(f32[27,195,4,1024]{3,2,1,0:T(4,128)} %multiply_reduce_fusion) | data formatting | bytes 172523520 | tf_op jit(solution)/shard_map/dot_general | solution.py:99
  242.2 73.9 %fusion.6 = f32[27,195,384]{2,1,0:T(8,128)S(1)} fusion(f32[27,195,4096]{2,1,0:T(8,128)} %dot_general.72, pred[4096,384,1]{1,0,2:T(32,128)(4,1)S(1)} %fusion.297), kind=kOutput, calls=%fused_computation.47 | convolution fusion | flops 99373547520 | bytes 95921664 | tf_op jit(solution)/shard_map/dot_general | solution.py:99
  332.1 11.5 collective-permute-done.1
  344.8 9.8 convolution_bitcast_fusion
  354.7 9.7 negate_bitcast_fusion
  369.8 4.2 pad_maximum_fusion
  374.1 11.4 copy.133
  385.5 80.2 %all_to_all.50 = f32[2,192,4608]{2,0,1:T(2,128)S(1)} all-to-all(f32[2,192,4608]{2,0,1:T(2,128)} %copy.133), channel_id=1, replica_groups=mesh['gz'=16,'gy'=2] {'gy'}, dimensions={1} | all-to-all | bytes 14155776 | tf_op jit(solution)/shard_map/all_to_all | solution.py:162
  476.7 10.3 fusion.44
  486.9 5.5 copy.137
  496.4 10.2 fusion.42
  506.7 10.9 multiply_subtract_fusion
  520.9 14.3 %multiply_add_fusion = f32[384,96,24]{0,1,2:T(8,128)} fusion(f32[384,96,24]{0,1,2:T(8,128)} %fusion.42, f32[96,384,24]{1,0,2:T(8,128)} %copy-done.2), kind=kOutput, calls=%fused_computation.63 | convolution fusion | flops 4079960064 | bytes 10616832 | tf_op jit(solution)/shard_map/xyz,yk->kzx/dot_general | solution.py:75
  535.2 5.3 copy.142
  554.9 5.1 all-to-all-start.1
  563.0 124.8 %all-to-all-done.1 = f32[16,2,24,2304]{3,2,1,0:T(8,128)} async-done(((f32[16,2,24,2304]{3,2,1,0:T(8,128)}), f32[16,2,24,2304]{3,2,1,0:T(8,128)}, u32[]{:S(2)}, u32[]{:S(2)}) %all-to-all-start.1) | async-done | bytes 7077920 | tf_op jit(solution)/shard_map/all_to_all | solution.py:170
  694.2 6.2 squeeze.37
  700.4 15.8 %fusion.40 = f32[24,96,384]{2,1,0:T(8,128)} fusion(f32[24,384,96]{2,1,0:T(8,128)} %squeeze.37), kind=kOutput, calls=%fused_computation.101 | convolution fusion | flops 4078190592 | bytes 7077888 | tf_op jit(solution)/shard_map/yzx,zk->yxk/dot_general | solution.py:72
  719.0 6.4 squeeze.38
  725.4 15.0 %fusion.38 = f32[24,96,384]{2,1,0:T(8,128)S(1)} fusion(f32[24,384,96]{2,1,0:T(8,128)} %squeeze.38), kind=kOutput, calls=%fused_computation.99 | convolution fusion | flops 4078190592 | bytes 7077888 | tf_op jit(solution)/shard_map/yzx,zk->yxk/dot_general | solution.py:74
  740.5 14.8 %subtract_multiply_fusion = f32[24,96,384]{2,1,0:T(8,128)S(1)} fusion(f32[24,96,384]{2,1,0:T(8,128)S(1)} %copy-done.9, f32[24,384,96]{2,1,0:T(8,128)} %squeeze.38, f32[96]{0:T(128)S(1)} %copy-done.41, f32[24,384]{1,0:T(8,128)S(1)} %copy-done.11, pred[96]{0:T(512)(128)(4,1)S(1)} %copy-done.42, pred[24,384]{1,0:T(8,128)(4,1)S(1)} %broadcast_or_fusion, ...), kind=kOutput, calls=%fused_computation.62 | convolution fusion | flops 4091461632 | bytes 10700640 | tf_op jit(solution)/shard_map/yzx,zk->yxk/dot_general | solution.py:73
  755.4 12.5 add_multiply_fusion.1
  767.8 9.2 fusion.48
  777.1 10.7 fusion.46
  787.7 10.7 convolution_subtract_fusion
  798.5 8.9 copy.149
  807.4 13.8 %convolution_add_fusion = f32[384,24,96]{0,2,1:T(8,128)} fusion(f32[384,24,96]{0,2,1:T(8,128)} %fusion.46, f32[24,96,384]{2,1,0:T(8,128)S(1)} %subtract_multiply_fusion, s32[384]{0:T(512)S(1)} %add_select_fusion.7), kind=kOutput, calls=%fused_computation.76 | convolution fusion | flops 4079075328 | bytes 10618368 | tf_op jit(solution)/shard_map/yxk,kp->pyx/dot_general | solution.py:75
  821.2 9.3 copy.150
  830.5 11.2 pad_maximum_fusion.1
  841.8 31.3 %all-to-all-start.2 = ((f32[2,384,2304]{2,0,1:T(2,128)}), f32[2,384,2304]{2,0,1:T(2,128)}, u32[]{:S(2)}, u32[]{:S(2)}) async-start(f32[2,384,2304]{2,0,1:T(2,128)} %pad_maximum_fusion.1), calls=%async_computation.2 | async-start | bytes 14155776 | tf_op jit(solution)/shard_map/all_to_all | solution.py:194
  873.2 127.6 %all-to-all-done.2 = f32[2,384,2304]{2,0,1:T(2,128)} async-done(((f32[2,384,2304]{2,0,1:T(2,128)}), f32[2,384,2304]{2,0,1:T(2,128)}, u32[]{:S(2)}, u32[]{:S(2)}) %all-to-all-start.2) | async-done | bytes 7077920 | tf_op jit(solution)/shard_map/all_to_all | solution.py:194
  1007.8 4.5 squeeze.40
  1016.5 10.3 fusion.80
  1026.7 10.4 fusion.74
  1038.2 4.5 squeeze.39
  1046.7 9.3 fusion.76
  1056.0 9.7 fusion.78
  1074.1 12.3 copy.160
  1086.4 6.8 all-to-all-start.3
  1095.1 77.8 %all-to-all-done.3 = f32[2,384,2304]{2,0,1:T(2,128)} async-done(((f32[2,384,2304]{2,0,1:T(2,128)}), f32[2,384,2304]{2,0,1:T(2,128)}, u32[]{:S(2)}, u32[]{:S(2)}) %all-to-all-start.3) | async-done | bytes 7077920 | tf_op jit(solution)/shard_map/all_to_all | solution.py:207
  1178.8 5.5 copy.164
  1187.9 12.9 %fusion.8 = f32[384,192,24]{0,1,2:T(8,128)S(1)} fusion(f32[192,192,24]{0,2,1:T(8,128)} %bitcast.217, f32[192]{0:T(256)S(1)} %compare_select_fusion.3), kind=kOutput, calls=%fused_computation.48 | convolution fusion | flops 4077600768 | bytes 10617600 | tf_op jit(solution)/shard_map/ykz,xk->zyx/dot_general | solution.py:213
  1200.9 10.8 multiply_bitcast_fusion
  1212.1 5.6 collective-permute-done.2
  1217.8 27.0 %collective-permute-start.3 = (f32[3,195,384]{2,1,0:T(8,128)S(1)}, f32[3,195,384]{2,1,0:T(8,128)S(1)}, u32[]{:S(2)}, u32[]{:S(2)}) collective-permute-start(f32[3,195,384]{2,1,0:T(8,128)S(1)} %pad_maximum_fusion.3), channel_id=1, source_target_pairs={{2,0},{4,2},{6,4},{8,6},{10,8},{12,10},{14,12},{16,14},{18,16},{20... | collective-permute-start | bytes 2695688 | tf_op jit(solution)/shard_map/ppermute | solution.py:16
  1245.9 9.8 collective-permute-done.3
  1255.8 11.8 fusion
  (191 shorter events, 114.6 us)
Async XLA Ops:
  165.2 75.9 %copy-start.12 = (s32[1,1024]{1,0:T(1,128)S(1)}, s32[1,1024]{1,0:T(1,128)}, u32[]{:S(2)}) copy-start(s32[1,1024]{1,0:T(1,128)} %get-tuple-element.46) | copy-start | bytes 12292
  316.1 7.3 collective-permute-start
  328.3 15.2 %collective-permute-start.1 = (f32[3,192,384]{2,1,0:T(8,128)S(1)}, f32[3,192,384]{2,1,0:T(8,128)S(1)}, u32[]{:S(2)}, u32[]{:S(2)}) collective-permute-start(f32[3,192,384]{2,1,0:T(8,128)S(1)} %slice.168), channel_id=1, source_target_pairs={{30,0},{0,2},{2,4},{4,6},{6,8},{8,10},{10,12},{12,14},{14,16},{16,... | collective-permute-start | bytes 2654216 | tf_op jit(solution)/shard_map/ppermute | solution.py:16
  476.6 10.3 copy-start.2
  496.4 10.2 copy-start.3
  554.9 132.8 %all-to-all-start.1 = ((f32[16,2,24,2304]{3,2,1,0:T(8,128)}), f32[16,2,24,2304]{3,2,1,0:T(8,128)}, u32[]{:S(2)}, u32[]{:S(2)}) async-start(f32[16,2,24,2304]{3,2,1,0:T(8,128)} %fusion.102), calls=%async_computation.1 | async-start | bytes 14155776 | tf_op jit(solution)/shard_map/all_to_all | solution.py:170
  725.4 15.1 %copy-start.9 = (f32[24,96,384]{2,1,0:T(8,128)S(1)}, f32[24,96,384]{2,1,0:T(8,128)}, u32[]{:S(2)}) copy-start(f32[24,96,384]{2,1,0:T(8,128)} %fusion.40) | copy-start | bytes 10616836
  725.4 15.1 %copy-start.10 = (f32[24,384]{1,0:T(8,128)S(1)}, f32[24,384]{1,0:T(8,128)}, u32[]{:S(2)}) copy-start(f32[24,384]{1,0:T(8,128)} %broadcast_add_fusion) | copy-start | bytes 110596
  725.4 15.1 %copy-start.11 = (f32[24,384]{1,0:T(8,128)S(1)}, f32[24,384]{1,0:T(8,128)}, u32[]{:S(2)}) copy-start(f32[24,384]{1,0:T(8,128)} %broadcast_multiply_fusion) | copy-start | bytes 110596
  725.4 15.1 %copy-start.40 = (f32[96]{0:T(128)S(1)}, f32[96]{0:T(128)}, u32[]{:S(2)}) copy-start(f32[96]{0:T(128)} %get-tuple-element.81) | copy-start | bytes 1156
  725.4 15.1 %copy-start.41 = (f32[96]{0:T(128)S(1)}, f32[96]{0:T(128)}, u32[]{:S(2)}) copy-start(f32[96]{0:T(128)} %get-tuple-element.82) | copy-start | bytes 1156
  725.4 15.1 %copy-start.42 = (pred[96]{0:T(512)(128)(4,1)S(1)}, pred[96]{0:T(512)(128)(4,1)}, u32[]{:S(2)}) copy-start(pred[96]{0:T(512)(128)(4,1)} %fusion.206) | copy-start | bytes 292
  725.4 29.9 %slice-start = ((s8[4718592]{0:T(1024)(128)(4,1)}), s8[4194304]{0:T(1024)(128)(4,1)S(1)}, s32[]{:S(2)}) async-start(s8[4718592]{0:T(1024)(128)(4,1)} %bitcast.218), calls=%async_computation.4 | async-start | bytes 8388608
  740.5 14.8 %slice-start.1 = ((s8[4718592]{0:T(1024)(128)(4,1)}), s8[524288]{0:T(1024)(128)(4,1)S(1)}, s32[]{:S(2)}) async-start(s8[4718592]{0:T(1024)(128)(4,1)} %bitcast.218), calls=%async_computation.5 | async-start | bytes 1048576
  821.2 9.3 copy-start.6
  841.8 159.0 %all-to-all-start.2 = ((f32[2,384,2304]{2,0,1:T(2,128)}), f32[2,384,2304]{2,0,1:T(2,128)}, u32[]{:S(2)}, u32[]{:S(2)}) async-start(f32[2,384,2304]{2,0,1:T(2,128)} %pad_maximum_fusion.1), calls=%async_computation.2 | async-start | bytes 14155776 | tf_op jit(solution)/shard_map/all_to_all | solution.py:194
  1026.7 10.4 copy-start.5
  1056.0 9.7 copy-start.8
  1086.4 6.8 copy-start.38
  1086.4 7.4 copy-start.13
  1086.4 86.5 %all-to-all-start.3 = ((f32[2,384,2304]{2,0,1:T(2,128)}), f32[2,384,2304]{2,0,1:T(2,128)}, u32[]{:S(2)}, u32[]{:S(2)}) async-start(f32[2,384,2304]{2,0,1:T(2,128)} %copy.160), calls=%async_computation.3 | async-start | bytes 14155776 | tf_op jit(solution)/shard_map/all_to_all | solution.py:207
  1187.9 12.9 %copy-start.4 = (f32[1,192,2,2304]{1,3,2,0:T(8,128)S(1)}, f32[1,192,2,2304]{1,3,2,0:T(8,128)}, u32[]{:S(2)}) copy-start(f32[1,192,2,2304]{1,3,2,0:T(8,128)} %copy.162) | copy-start | bytes 10616836
  1200.8 11.0 copy-start.29
  1200.8 11.0 copy-start.30
  1200.9 11.0 copy-start.31
  1200.9 11.0 copy-start.32
  1200.9 11.0 copy-start.33
  1200.9 11.0 copy-start.34
  1200.9 11.0 copy-start.35
  1200.9 11.0 copy-start.36
  1211.8 5.9 collective-permute-start.2
  1211.9 33.2 %copy-start.16 = (f32[1,128]{1,0:T(1,128)S(1)}, f32[1,128]{1,0:T(1,128)}, u32[]{:S(2)}) copy-start(f32[1,128]{1,0:T(1,128)} %get-tuple-element.71) | copy-start | bytes 1540
  1212.0 33.2 %copy-start.22 = (f32[1,128]{1,0:T(1,128)S(1)}, f32[1,128]{1,0:T(1,128)}, u32[]{:S(2)}) copy-start(f32[1,128]{1,0:T(1,128)} %get-tuple-element.57) | copy-start | bytes 1540
  1212.0 33.2 %copy-start.23 = (f32[1,128]{1,0:T(1,128)S(1)}, f32[1,128]{1,0:T(1,128)}, u32[]{:S(2)}) copy-start(f32[1,128]{1,0:T(1,128)} %get-tuple-element.58) | copy-start | bytes 1540
  1212.0 33.2 %copy-start.24 = (f32[1,128]{1,0:T(1,128)S(1)}, f32[1,128]{1,0:T(1,128)}, u32[]{:S(2)}) copy-start(f32[1,128]{1,0:T(1,128)} %get-tuple-element.59) | copy-start | bytes 1540
  1212.0 33.2 %copy-start.25 = (f32[1,128]{1,0:T(1,128)S(1)}, f32[1,128]{1,0:T(1,128)}, u32[]{:S(2)}) copy-start(f32[1,128]{1,0:T(1,128)} %get-tuple-element.63) | copy-start | bytes 1540
  1212.0 33.2 %copy-start.26 = (f32[1,128]{1,0:T(1,128)S(1)}, f32[1,128]{1,0:T(1,128)}, u32[]{:S(2)}) copy-start(f32[1,128]{1,0:T(1,128)} %get-tuple-element.64) | copy-start | bytes 1540
  1212.0 33.2 %copy-start.27 = (f32[1,128]{1,0:T(1,128)S(1)}, f32[1,128]{1,0:T(1,128)}, u32[]{:S(2)}) copy-start(f32[1,128]{1,0:T(1,128)} %get-tuple-element.65) | copy-start | bytes 1540
  1212.0 33.2 %copy-start.28 = (f32[1,128]{1,0:T(1,128)S(1)}, f32[1,128]{1,0:T(1,128)}, u32[]{:S(2)}) copy-start(f32[1,128]{1,0:T(1,128)} %get-tuple-element.66) | copy-start | bytes 1540
  1212.0 33.2 %copy-start.14 = (f32[1,128]{1,0:T(1,128)S(1)}, f32[1,128]{1,0:T(1,128)}, u32[]{:S(2)}) copy-start(f32[1,128]{1,0:T(1,128)} %get-tuple-element.73) | copy-start | bytes 1540
  1212.0 33.2 %copy-start.15 = (f32[1,128]{1,0:T(1,128)S(1)}, f32[1,128]{1,0:T(1,128)}, u32[]{:S(2)}) copy-start(f32[1,128]{1,0:T(1,128)} %get-tuple-element.75) | copy-start | bytes 1540
  1212.0 33.2 %copy-start.17 = (f32[1,128]{1,0:T(1,128)S(1)}, f32[1,128]{1,0:T(1,128)}, u32[]{:S(2)}) copy-start(f32[1,128]{1,0:T(1,128)} %get-tuple-element.49) | copy-start | bytes 1540
  1212.1 33.2 %copy-start.18 = (f32[1,128]{1,0:T(1,128)S(1)}, f32[1,128]{1,0:T(1,128)}, u32[]{:S(2)}) copy-start(f32[1,128]{1,0:T(1,128)} %get-tuple-element.60) | copy-start | bytes 1540
  1212.1 33.2 %copy-start.19 = (f32[1,128]{1,0:T(1,128)S(1)}, f32[1,128]{1,0:T(1,128)}, u32[]{:S(2)}) copy-start(f32[1,128]{1,0:T(1,128)} %get-tuple-element.61) | copy-start | bytes 1540
  1212.1 33.2 %copy-start.20 = (f32[1,128]{1,0:T(1,128)S(1)}, f32[1,128]{1,0:T(1,128)}, u32[]{:S(2)}) copy-start(f32[1,128]{1,0:T(1,128)} %get-tuple-element.62) | copy-start | bytes 1540
  1212.1 33.2 %copy-start.21 = (f32[1,128]{1,0:T(1,128)S(1)}, f32[1,128]{1,0:T(1,128)}, u32[]{:S(2)}) copy-start(f32[1,128]{1,0:T(1,128)} %get-tuple-element.67) | copy-start | bytes 1540
  1212.1 33.2 %copy-start.37 = (s32[128]{0:T(128)S(1)}, s32[128]{0:T(128)}, u32[]{:S(2)}) copy-start(s32[128]{0:T(128)} %get-tuple-element.68) | copy-start | bytes 1540
  1217.8 38.0 %collective-permute-start.3 = (f32[3,195,384]{2,1,0:T(8,128)S(1)}, f32[3,195,384]{2,1,0:T(8,128)S(1)}, u32[]{:S(2)}, u32[]{:S(2)}) collective-permute-start(f32[3,195,384]{2,1,0:T(8,128)S(1)} %pad_maximum_fusion.3), channel_id=1, source_target_pairs={{2,0},{4,2},{6,4},{8,6},{10,8},{12,10},{14,12},{16,14},{18,16},{20... | collective-permute-start | bytes 2695688 | tf_op jit(solution)/shard_map/ppermute | solution.py:16
  (4 other events, 11.2 us)
